TPU v7x, 32 devices: a whole 2x2x4 slice. The times are simulated.
32 devices in a mesh: batch: 4 (over z), head: 4 (over y, x), ctx: 2 (over core).
Axes of the slice: x: 2, y: 2, z: 4, core: 2. Of those that a mesh axis runs over, the one named last changes fastest.
Arguments:
- hidden_in: bfloat16 [4, 1024, 960], P('batch', 'ctx'), may hold values from -6 to 6
- cotangent: bfloat16 [4, 1024, 960], P('batch', 'ctx'), may hold values from -6 to 6
- lengths: int32 [4], P('batch'), may hold values from 64 to 1024, as said below
- owners: int32 [5], replicated, may hold values from 0 to 3, as said below
- w_query: bfloat16 [960, 960], replicated, may hold values from -0.1875 to 0.1875
- w_key: bfloat16 [960, 320], replicated, may hold values from -0.1875 to 0.1875
- w_value: bfloat16 [960, 320], replicated, may hold values from -0.1875 to 0.1875
- w_output: bfloat16 [960, 960], replicated, may hold values from -2 to 2
- gate_weight: bfloat16 [960, 2560], P(None, 'head'), may hold values from -0.1875 to 0.1875
- up_weight: bfloat16 [960, 2560], P(None, 'head'), may hold values from -0.1875 to 0.1875
- down_weight: bfloat16 [2560, 960], P('head'), may hold values from -0.125 to 0.125
- gain_attn: float32 [960], replicated, may hold values from 0.1 to 1.9
- gain_ffn: float32 [960], replicated, may hold values from 0.1 to 1.9
Outputs:
- output: bfloat16 [4, 1024, 960], P('batch', 'ctx')
- grad_input: float32 [4, 1024, 960], P('batch', 'ctx')
- grad_query: float32 [960, 1536], P(None, 'head')
- grad_key: float32 [960, 512], P(None, 'head')
- grad_value: float32 [960, 512], P(None, 'head')
- grad_output: float32 [1536, 960], P('head')
- grad_gate: float32 [960, 2560], P(None, 'head')
- grad_up: float32 [960, 2560], P(None, 'head')
- grad_down: float32 [2560, 960], P('head')
- grad_gain_attn: float32 [960], replicated
- grad_gain_ffn: float32 [960], replicated
Inputs may be any that keep to these rules, and one draw needn't show every extreme that they name: `lengths`: at least one sequence has all 1024 slots valid. `owners`: every head index computes one or two groups.
All inputs are finite; a program needn't handle non-finite values.
Results may differ from a plain program's by a relative error of at most 0.034.
Values may be sent and summed in bfloat16 or wider, within the bound.
A program may use at most 192 MiB of HBM per device.

v0:
```python
import math

import jax
import jax.numpy as jnp
from jax import lax
from jax.sharding import PartitionSpec as P

KV = 5
HD = 64
GQ = 3


EPSILON = 1e-05
MASKED_OUT = -1e30


def from_behind(value, axis, steps):
    count = lax.axis_size(axis)
    first, last = (max(0, -steps), min(count, count - steps))
    return lax.ppermute(value, axis, [(source, source + steps) for source in range(first, last)])


def rms_normed(residual, gain_vec):
    inv_rms = lax.rsqrt(jnp.mean(residual * residual, axis=-1, keepdims=True) + EPSILON)
    return residual * inv_rms * gain_vec


def rope_tables(positions):
    steps_half = jnp.arange(HD // 2, dtype=jnp.float32)
    inverse = jnp.exp(steps_half * (-2.0 * math.log(10000.0) / HD))
    angles = positions.astype(jnp.float32)[:, None] * inverse[None, :]
    return (jnp.cos(angles), jnp.sin(angles))


def rotate(tensor, cos_tab, sin_tab):
    half_width = tensor.shape[-1] // 2
    first_half = tensor[..., :half_width]
    second_half = tensor[..., half_width:]
    return jnp.concatenate(
        [
            first_half * cos_tab - second_half * sin_tab,
            second_half * cos_tab + first_half * sin_tab,
        ],
        axis=-1,
    )


def unrotate(tensor, cos_tab, sin_tab):
    half_width = tensor.shape[-1] // 2
    first_half = tensor[..., :half_width]
    second_half = tensor[..., half_width:]
    return jnp.concatenate(
        [
            first_half * cos_tab + second_half * sin_tab,
            second_half * cos_tab - first_half * sin_tab,
        ],
        axis=-1,
    )


def silu_product(gate_preactivation, up_preactivation):
    return jax.nn.silu(gate_preactivation) * up_preactivation


def slot_weights(owners, w_query, w_key, w_value, w_output):
    device = lax.axis_index("head")
    owned_mask = (owners == device).astype(jnp.int32)
    ranked = jnp.cumsum(owned_mask) - 1
    group_width = GQ * HD
    query_cols, key_cols, value_cols, out_rows = ([], [], [], [])
    for which_slot in range(2):
        chosen = owned_mask * (ranked == which_slot).astype(jnp.int32)
        present = jnp.sum(chosen).astype(w_query.dtype)
        group_id = jnp.sum(chosen * jnp.arange(KV, dtype=jnp.int32))
        query_cols.append(
            lax.dynamic_slice_in_dim(w_query, group_id * group_width, group_width, 1) * present
        )
        key_cols.append(lax.dynamic_slice_in_dim(w_key, group_id * HD, HD, 1) * present)
        value_cols.append(lax.dynamic_slice_in_dim(w_value, group_id * HD, HD, 1) * present)
        out_rows.append(
            lax.dynamic_slice_in_dim(w_output, group_id * group_width, group_width, 0) * present
        )
    input_weight = jnp.concatenate(query_cols + key_cols + value_cols, axis=1)
    return (input_weight, jnp.concatenate(out_rows, axis=0))


def masked_scores(queries, keys_all, allowed):
    score_scale = HD ** (-0.5)
    raw_scores = (
        jnp.einsum("bqsge,bkse->bsgqk", queries, keys_all, preferred_element_type=jnp.float32)
        * score_scale
    )
    return jnp.where(allowed[:, None, None], raw_scores, MASKED_OUT)


def forward_pass(residual, valid_rows, allowed, tables, weights):
    input_weight, output_weight, gate_weight, up_weight, down_weight, gain_attn, gain_ffn = weights
    cos_tab, sin_tab = tables
    batch_rows, half_rows = (residual.shape[0], residual.shape[1])
    group_width = GQ * HD
    attention_normalized = rms_normed(residual, gain_attn).astype(jnp.bfloat16)
    projected_rows = jnp.einsum(
        "pjm,mx->pjx", attention_normalized, input_weight, preferred_element_type=jnp.float32
    )
    query_pre = projected_rows[..., : 2 * group_width].reshape(batch_rows, half_rows, 2, GQ, HD)
    key_pre = projected_rows[..., 2 * group_width : 2 * group_width + 2 * HD].reshape(
        batch_rows, half_rows, 2, HD
    )
    queries = rotate(query_pre, cos_tab[:, None, None, :], sin_tab[:, None, None, :]).astype(
        jnp.bfloat16
    )
    keys_local = (
        rotate(key_pre, cos_tab[:, None, :], sin_tab[:, None, :])
        .astype(jnp.bfloat16)
        .reshape(batch_rows, half_rows, 2 * HD)
    )
    values_local = projected_rows[..., 2 * group_width + 2 * HD :].astype(jnp.bfloat16)
    received = from_behind(jnp.stack([keys_local, values_local]), "ctx", 1)
    keys_all = jnp.concatenate([received[0], keys_local], axis=1).reshape(
        batch_rows, 2 * half_rows, 2, HD
    )
    values_all = jnp.concatenate([received[1], values_local], axis=1).reshape(
        batch_rows, 2 * half_rows, 2, HD
    )
    masked = masked_scores(queries, keys_all, allowed)
    row_peak = jnp.max(masked, axis=-1, keepdims=True)
    exp_scores = jnp.exp(masked - row_peak)
    exp_total = jnp.sum(exp_scores, axis=-1, keepdims=True)
    soft_probs = (exp_scores / exp_total).astype(jnp.bfloat16)
    log_norm = row_peak + jnp.log(exp_total)
    attention_result = jnp.einsum(
        "bsgqk,bkse->bqsge", soft_probs, values_all, preferred_element_type=jnp.float32
    )
    attention_result = attention_result.reshape(batch_rows, half_rows, 2 * group_width).astype(
        jnp.bfloat16
    )
    attention_portion = jnp.einsum(
        "ekh,hr->ekr", attention_result, output_weight, preferred_element_type=jnp.float32
    )
    attn_total = lax.psum(attention_portion.astype(jnp.bfloat16), "head").astype(jnp.float32)
    middle = residual + attn_total
    feedforward_normalized = rms_normed(middle, gain_ffn).astype(jnp.bfloat16)
    gate_preactivation = jnp.einsum(
        "igy,yl->igl", feedforward_normalized, gate_weight, preferred_element_type=jnp.float32
    )
    up_preactivation = jnp.einsum(
        "igy,yl->igl", feedforward_normalized, up_weight, preferred_element_type=jnp.float32
    )
    activation_values = silu_product(gate_preactivation, up_preactivation).astype(jnp.bfloat16)
    feedforward_portion = jnp.einsum(
        "pwc,ci->pwi", activation_values, down_weight, preferred_element_type=jnp.float32
    )
    ffn_total = lax.psum(feedforward_portion.astype(jnp.bfloat16), "head").astype(jnp.float32)
    result = valid_rows * (middle + ffn_total)
    saved_state = (
        residual,
        attention_normalized,
        queries,
        keys_all,
        values_all,
        log_norm,
        attention_result,
        middle,
        feedforward_normalized,
        gate_preactivation,
        up_preactivation,
        activation_values,
    )
    return (result, saved_state)


def backward_pass(d_result, saved_state, valid_rows, allowed, tables, weights, grads):
    (
        residual,
        attention_normalized,
        queries,
        keys_all,
        values_all,
        log_norm,
        attention_result,
        middle,
        feedforward_normalized,
        gate_preactivation,
        up_preactivation,
        activation_values,
    ) = saved_state
    input_weight, output_weight, gate_weight, up_weight, down_weight, gain_attn, gain_ffn = weights
    g_in, output_gradient, g_gate, up_weight_gradient, g_down, g_gain_attn, g_gain_ffn = grads
    cos_tab, sin_tab = tables
    batch_rows, half_rows = (residual.shape[0], residual.shape[1])
    group_width = GQ * HD
    score_scale = HD ** (-0.5)
    d_pre = valid_rows * d_result
    feedforward_gradient = d_pre.astype(jnp.bfloat16)
    activation_gradient = jnp.einsum(
        "wuc,kc->wuk", feedforward_gradient, down_weight, preferred_element_type=jnp.float32
    )
    g_down = g_down + jnp.einsum(
        "evu,evo->uo", activation_values, feedforward_gradient, preferred_element_type=jnp.float32
    )
    _, pull_ffn = jax.vjp(silu_product, gate_preactivation, up_preactivation)
    d_gate_full, d_up_full = pull_ffn(activation_gradient)
    gate_gradient = d_gate_full.astype(jnp.bfloat16)
    up_gradient = d_up_full.astype(jnp.bfloat16)
    g_gate = g_gate + jnp.einsum(
        "rkh,rkg->hg", feedforward_normalized, gate_gradient, preferred_element_type=jnp.float32
    )
    up_weight_gradient = up_weight_gradient + jnp.einsum(
        "rkh,rkg->hg", feedforward_normalized, up_gradient, preferred_element_type=jnp.float32
    )
    feedforward_addend = jnp.einsum(
        "hgu,pu->hgp", gate_gradient, gate_weight, preferred_element_type=jnp.float32
    )
    feedforward_addend = feedforward_addend + jnp.einsum(
        "hgu,pu->hgp", up_gradient, up_weight, preferred_element_type=jnp.float32
    )
    d_normed_ffn = lax.psum(feedforward_addend.astype(jnp.bfloat16), "head").astype(jnp.float32)
    _, pull_second = jax.vjp(rms_normed, middle, gain_ffn)
    d_middle_norm, d_gain_ffn = pull_second(d_normed_ffn)
    g_gain_ffn = g_gain_ffn + d_gain_ffn
    d_middle = d_pre + d_middle_norm
    attention_gradient = d_middle.astype(jnp.bfloat16)
    output_gradient = output_gradient + jnp.einsum(
        "yfj,yfw->jw", attention_result, attention_gradient, preferred_element_type=jnp.float32
    )
    attention_result_gradient = jnp.einsum(
        "osw,tw->ost", attention_gradient, output_weight, preferred_element_type=jnp.float32
    )
    attention_result_gradient = attention_result_gradient.astype(jnp.bfloat16).reshape(
        batch_rows, half_rows, 2, GQ, HD
    )
    masked = masked_scores(queries, keys_all, allowed)
    soft_probs = jnp.exp(masked - log_norm)
    d_probs = jnp.einsum(
        "bqsge,bkse->bsgqk",
        attention_result_gradient,
        values_all,
        preferred_element_type=jnp.float32,
    )
    d_values_all = jnp.einsum(
        "bsgqk,bqsge->bkse",
        soft_probs.astype(jnp.bfloat16),
        attention_result_gradient,
        preferred_element_type=jnp.float32,
    )
    row_delta = jnp.sum(soft_probs * d_probs, axis=-1, keepdims=True)
    d_scores = (soft_probs * (d_probs - row_delta)).astype(jnp.bfloat16)
    d_queries = (
        jnp.einsum("bsgqk,bkse->bqsge", d_scores, keys_all, preferred_element_type=jnp.float32)
        * score_scale
    )
    d_keys_all = (
        jnp.einsum("bsgqk,bqsge->bkse", d_scores, queries, preferred_element_type=jnp.float32)
        * score_scale
    )
    remote = jnp.stack([d_keys_all[:, :half_rows], d_values_all[:, :half_rows]]).reshape(
        2, batch_rows, half_rows, 2 * HD
    )
    returned = from_behind(remote.astype(jnp.bfloat16), "ctx", -1).astype(remote.dtype)
    d_keys = d_keys_all[:, half_rows:] + returned[0].reshape(batch_rows, half_rows, 2, HD)
    d_values = d_values_all[:, half_rows:].reshape(batch_rows, half_rows, 2 * HD) + returned[1]
    d_query_pre = unrotate(d_queries, cos_tab[:, None, None, :], sin_tab[:, None, None, :]).astype(
        jnp.bfloat16
    )
    d_key_pre = unrotate(d_keys, cos_tab[:, None, :], sin_tab[:, None, :]).astype(jnp.bfloat16)
    projection_gradient = jnp.concatenate(
        [
            d_query_pre.reshape(batch_rows, half_rows, 2 * group_width),
            d_key_pre.reshape(batch_rows, half_rows, 2 * HD),
            d_values.astype(jnp.bfloat16),
        ],
        axis=-1,
    )
    g_in = g_in + jnp.einsum(
        "vtx,vto->xo", attention_normalized, projection_gradient, preferred_element_type=jnp.float32
    )
    attention_addend = jnp.einsum(
        "xkr,vr->xkv", projection_gradient, input_weight, preferred_element_type=jnp.float32
    )
    d_normed_attn = lax.psum(attention_addend.astype(jnp.bfloat16), "head").astype(jnp.float32)
    _, pull_first = jax.vjp(rms_normed, residual, gain_attn)
    d_resid_norm, d_gain_attn = pull_first(d_normed_attn)
    g_gain_attn = g_gain_attn + d_gain_attn
    return (
        d_middle + d_resid_norm,
        (g_in, output_gradient, g_gate, up_weight_gradient, g_down, g_gain_attn, g_gain_ffn),
    )


def body(
    hidden_in,
    cotangent,
    lengths,
    owners,
    w_query,
    w_key,
    w_value,
    w_output,
    gate_weight,
    up_weight,
    down_weight,
    gain_attn,
    gain_ffn,
):
    half_rows = hidden_in.shape[1]
    group_width = GQ * HD
    input_weight, output_weight = slot_weights(owners, w_query, w_key, w_value, w_output)
    ctx_place = lax.axis_index("ctx")
    local_pos = ctx_place * half_rows + jnp.arange(half_rows, dtype=jnp.int32)
    key_pos = (ctx_place - 1) * half_rows + jnp.arange(2 * half_rows, dtype=jnp.int32)
    allowed = (
        (key_pos[None, None, :] <= local_pos[None, :, None])
        & (key_pos[None, None, :] >= 0)
        & (key_pos[None, None, :] < lengths[:, None, None])
    )
    valid_rows = (local_pos[None, :] < lengths[:, None]).astype(jnp.float32)[..., None]
    tables = rope_tables(local_pos)
    weights = (
        input_weight,
        output_weight,
        gate_weight,
        up_weight,
        down_weight,
        gain_attn,
        gain_ffn,
    )
    first_out, first_saved = forward_pass(
        hidden_in.astype(jnp.float32), valid_rows, allowed, tables, weights
    )
    second_out, second_saved = forward_pass(first_out, valid_rows, allowed, tables, weights)
    zero_grads = (
        jnp.zeros(input_weight.shape, jnp.float32),
        jnp.zeros(output_weight.shape, jnp.float32),
        jnp.zeros(gate_weight.shape, jnp.float32),
        jnp.zeros(up_weight.shape, jnp.float32),
        jnp.zeros(down_weight.shape, jnp.float32),
        jnp.zeros(gain_attn.shape, jnp.float32),
        jnp.zeros(gain_ffn.shape, jnp.float32),
    )
    d_middle, grads = backward_pass(
        cotangent.astype(jnp.float32),
        second_saved,
        valid_rows,
        allowed,
        tables,
        weights,
        zero_grads,
    )
    d_input, grads = backward_pass(
        d_middle, first_saved, valid_rows, allowed, tables, weights, grads
    )
    g_in, output_gradient, g_gate, up_weight_gradient, g_down, g_gain_attn, g_gain_ffn = grads
    shares = (
        lax.psum_scatter(g_in.astype(jnp.bfloat16), "ctx", scatter_dimension=0, tiled=True).astype(
            jnp.float32
        ),
        lax.psum_scatter(
            output_gradient.astype(jnp.bfloat16), "ctx", scatter_dimension=0, tiled=True
        ).astype(jnp.float32),
        lax.psum_scatter(
            g_gate.astype(jnp.bfloat16), "ctx", scatter_dimension=0, tiled=True
        ).astype(jnp.float32),
        lax.psum_scatter(
            up_weight_gradient.astype(jnp.bfloat16), "ctx", scatter_dimension=0, tiled=True
        ).astype(jnp.float32),
        lax.psum_scatter(
            g_down.astype(jnp.bfloat16), "ctx", scatter_dimension=0, tiled=True
        ).astype(jnp.float32),
        lax.psum_scatter(
            g_gain_attn.astype(jnp.bfloat16), "ctx", scatter_dimension=0, tiled=True
        ).astype(jnp.float32),
        lax.psum_scatter(
            g_gain_ffn.astype(jnp.bfloat16), "ctx", scatter_dimension=0, tiled=True
        ).astype(jnp.float32),
    )
    shares = (
        lax.psum(shares[0].astype(jnp.bfloat16), "batch").astype(jnp.float32),
        lax.psum(shares[1].astype(jnp.bfloat16), "batch").astype(jnp.float32),
        lax.psum(shares[2].astype(jnp.bfloat16), "batch").astype(jnp.float32),
        lax.psum(shares[3].astype(jnp.bfloat16), "batch").astype(jnp.float32),
        lax.psum(shares[4].astype(jnp.bfloat16), "batch").astype(jnp.float32),
        lax.psum(shares[5].astype(jnp.bfloat16), "batch").astype(jnp.float32),
        lax.psum(shares[6].astype(jnp.bfloat16), "batch").astype(jnp.float32),
    )
    g_in, output_gradient, g_gate, up_weight_gradient, g_down, g_gain_attn, g_gain_ffn = (
        lax.all_gather(shares[0].astype(jnp.bfloat16), "ctx", axis=0, tiled=True).astype(
            jnp.float32
        ),
        lax.all_gather(shares[1].astype(jnp.bfloat16), "ctx", axis=0, tiled=True).astype(
            jnp.float32
        ),
        lax.all_gather(shares[2].astype(jnp.bfloat16), "ctx", axis=0, tiled=True).astype(
            jnp.float32
        ),
        lax.all_gather(shares[3].astype(jnp.bfloat16), "ctx", axis=0, tiled=True).astype(
            jnp.float32
        ),
        lax.all_gather(shares[4].astype(jnp.bfloat16), "ctx", axis=0, tiled=True).astype(
            jnp.float32
        ),
        lax.all_gather(shares[5].astype(jnp.bfloat16), "ctx", axis=0, tiled=True).astype(
            jnp.float32
        ),
        lax.all_gather(shares[6].astype(jnp.bfloat16), "ctx", axis=0, tiled=True).astype(
            jnp.float32
        ),
    )
    grad_query = g_in[:, : 2 * group_width]
    grad_key = g_in[:, 2 * group_width : 2 * group_width + 2 * HD]
    grad_value = g_in[:, 2 * group_width + 2 * HD :]
    return (
        second_out.astype(jnp.bfloat16),
        d_input,
        grad_query,
        grad_key,
        grad_value,
        output_gradient,
        g_gate,
        up_weight_gradient,
        g_down,
        g_gain_attn,
        g_gain_ffn,
    )


def solution(mesh):
    in_specs = (
        P("batch", "ctx", None),
        P("batch", "ctx", None),
        P("batch"),
        P(),
        P(),
        P(),
        P(),
        P(),
        P(None, "head"),
        P(None, "head"),
        P("head", None),
        P(),
        P(),
    )
    out_specs = (
        P("batch", "ctx", None),
        P("batch", "ctx", None),
        P(None, "head"),
        P(None, "head"),
        P(None, "head"),
        P("head", None),
        P(None, "head"),
        P(None, "head"),
        P("head", None),
        P(),
        P(),
    )
    return jax.shard_map(body, mesh=mesh, in_specs=in_specs, out_specs=out_specs, check_vma=False)
```

profile of v0, /device:TPU:27, one launch (start us, length us, event | category | flops | bytes accessed | tf_op | source)
XLA Modules:
  0.0 779.8 jit_solution(4948889365251473662)
XLA Ops:
  20.2 3.6 concatenate.128
  40.5 3.3 fusion.146
  45.7 2.8 copy-done.1
  53.6 53.2 %all-reduce.18.cloned.1.call-done = bf16[1,512,960]{1,2,0:T(8,128)(2,1)} async-done(((bf16[1,512,960]{1,2,0:T(8,128)(2,1)}), bf16[1,512,960]{1,2,0:T(8,128)(2,1)}) %all-reduce.18.cloned.1.call-update) | async-done | bytes 983056 | tf_op jit(solution)/shard_map/psum | solution.py:140
  115.5 51.6 %all-reduce.20.cloned.1.call-done = bf16[1,512,960]{1,2,0:T(8,128)(2,1)} async-done(((bf16[1,512,960]{1,2,0:T(8,128)(2,1)}), bf16[1,512,960]{1,2,0:T(8,128)(2,1)}) %all-reduce.20.cloned.1.call-update) | async-done | bytes 983056 | tf_op jit(solution)/shard_map/psum | solution.py:153
  193.7 3.5 fusion.147
  199.0 2.9 copy-done.2
  207.3 52.2 %all-reduce.22.cloned.1.call-done = bf16[1,512,960]{1,2,0:T(8,128)(2,1)} async-done(((bf16[1,512,960]{1,2,0:T(8,128)(2,1)}), bf16[1,512,960]{1,2,0:T(8,128)(2,1)}) %all-reduce.22.cloned.1.call-update) | async-done | bytes 983056 | tf_op jit(solution)/shard_map/psum | solution.py:140
  271.4 50.8 %all-reduce.24.cloned.1.call-done = bf16[1,512,960]{1,2,0:T(8,128)(2,1)} async-done(((bf16[1,512,960]{1,2,0:T(8,128)(2,1)}), bf16[1,512,960]{1,2,0:T(8,128)(2,1)}) %all-reduce.24.cloned.1.call-update) | async-done | bytes 983056 | tf_op jit(solution)/shard_map/psum | solution.py:217
  322.3 3.1 fusion.36
  328.2 11.2 %fusion.3 = (f32[2,3,512]{2,1,0:T(4,128)S(1)}, f32[2,1024,512,3]{2,1,3,0:T(8,128)}) fusion(f32[1,2,3,512,1024]{3,4,2,1,0:T(8,128)} %copy-done.2, f32[2,3,512]{2,1,0:T(4,128)S(1)} %log_add_fusion.1, bf16[512,2,3,64]{0,3,2,1:T(8,128)(2,1)S(1)} %bitcast.336, bf16[1,512,2,64]{1,3,2,0:T(8,128)(2,1)S(1)} %bitcast.353, bf16[1,512,2,64]{1,3,2,0:T(8,128)(2,1)S(1)} %bitcast.357), kind=kOutput, calls=%fused_computation.9 | convolution fusion | flops 412611584 | bytes 25845760 | tf_op jit(solution)/shard_map/bqsge,bkse->bsgqk/dot_general | solution.py:234
  339.9 6.8 fusion.16
  352.2 2.8 collective-permute-start.2
  359.4 50.9 %all-reduce.26.cloned.1.call-done = bf16[1,512,960]{1,2,0:T(8,128)(2,1)} async-done(((bf16[1,512,960]{1,2,0:T(8,128)(2,1)}), bf16[1,512,960]{1,2,0:T(8,128)(2,1)}) %all-reduce.26.cloned.1.call-update) | async-done | bytes 983056 | tf_op jit(solution)/shard_map/psum | solution.py:280
  439.0 33.6 %all-reduce.28.cloned.1.call-done = bf16[1,512,960]{1,2,0:T(8,128)(2,1)} async-done(((bf16[1,512,960]{1,2,0:T(8,128)(2,1)}), bf16[1,512,960]{1,2,0:T(8,128)(2,1)}) %all-reduce.28.cloned.1.call-update) | async-done | bytes 983056 | tf_op jit(solution)/shard_map/psum | solution.py:217
  472.6 2.9 fusion.38
  479.3 10.7 %fusion = (f32[2,3,512]{2,1,0:T(4,128)S(1)}, f32[2,1024,512,3]{2,1,3,0:T(8,128)}) fusion(f32[1,2,3,512,1024]{3,4,2,1,0:T(8,128)} %copy-done.1, f32[2,3,512]{2,1,0:T(4,128)S(1)} %log_add_fusion, bf16[512,2,3,64]{0,3,2,1:T(8,128)(2,1)S(1)} %bitcast.332, bf16[1,512,2,64]{1,3,2,0:T(8,128)(2,1)S(1)} %bitcast.349, bf16[1,512,2,64]{1,3,2,0:T(8,128)(2,1)S(1)} %bitcast.351), kind=kOutput, calls=%fused_computation.4 | convolution fusion | flops 412611584 | bytes 25845760 | tf_op jit(solution)/shard_map/bqsge,bkse->bsgqk/dot_general | solution.py:234
  493.6 7.1 fusion.17
  505.1 3.7 collective-permute-start.3
  510.2 4.9 fusion.64
  523.7 12.5 %reduce-scatter.6.cloned.1.call-done = bf16[480,640]{1,0:T(8,128)(2,1)} async-done(((bf16[960,640]{1,0:T(8,128)(2,1)}), bf16[480,640]{1,0:T(8,128)(2,1)}) %reduce-scatter.6.cloned.1.call-update) | async-done | bytes 614416 | tf_op jit(solution)/shard_map/reduce_scatter | solution.py:354
  536.4 3.1 fusion.51
  541.4 109.1 %all-reduce.32.cloned.1.call-done = (bf16[480,640]{1,0:T(8,128)(2,1)}, bf16[192,960]{1,0:T(8,128)(2,1)}, bf16[320,960]{1,0:T(8,128)(2,1)}, bf16[480,640]{1,0:T(8,128)(2,1)}, bf16[480,640]{1,0:T(8,128)(2,1)}) async-done(((bf16[480,640]{1,0:T(8,128)(2,1)}, bf16[192,960]{1,0:T(8,128)(2,1)}, bf16[320,960]{1,0:T(8,128)(2,1)}, bf16[480,640]{1,0:T(8,128)(2,1)}, bf16[480,640]{1,0:T(8,128)(2,1)}), ...) | async-done | bytes 2826256 | tf_op jit(solution)/shard_map/psum | solution.py:377
  653.8 68.9 %all-reduce.30.cloned.1.call-done = (bf16[1,512,960]{1,2,0:T(8,128)(2,1)}, bf16[1,512,960]{1,2,0:T(8,128)(2,1)}) async-done(((bf16[1,512,960]{1,2,0:T(8,128)(2,1)}, bf16[1,512,960]{1,2,0:T(8,128)(2,1)}), (bf16[1,512,960]{1,2,0:T(8,128)(2,1)}, bf16[1,512,960]{1,2,0:T(8,128)(2,1)})) %all-reduce.30.cloned.1.call-update) | async-done | bytes 1966096 | tf_op jit(solution)/shard_map/psum | solution.py:153
  725.3 3.2 all-reduce.8
  728.7 6.4 all-reduce.5
  735.5 4.2 all-reduce.7
  740.8 3.0 multiply_convert_fusion
  749.5 2.9 convert_element_type.525
  752.4 2.9 convert_element_type.527
  755.3 2.8 all-gather.5.cloned.1.call-done
  761.5 8.6 %all-gather.11.cloned.1.call-done = bf16[640,960]{1,0:T(8,128)(2,1)} async-done(((bf16[320,960]{1,0:T(8,128)(2,1)}), bf16[640,960]{1,0:T(8,128)(2,1)}) %all-gather.11.cloned.1.call-update) | async-done | bytes 1228816 | tf_op jit(solution)/shard_map/all_gather | solution.py:398
  (427 shorter events, 168.6 us)
Async XLA Ops:
  7.2 106.3 %copy-start = (bf16[640,960]{0,1:T(8,128)(2,1)S(1)}, bf16[640,960]{0,1:T(8,128)(2,1)}, u32[]{:S(2)}) copy-start(bf16[640,960]{0,1:T(8,128)(2,1)} %param.23) | copy-start | bytes 3686404
  7.2 99.6 %all-reduce.18.cloned.1.call-start = ((), (), s32[]{:S(2)}) async-start(), calls=%async_computation.5 | async-start | bytes 1966080 | tf_op jit(solution)/shard_map/psum | solution.py:140
  27.9 12.6 %copy-start.53 = (bf16[1,512,2,64]{1,3,2,0:T(8,128)(2,1)}, bf16[1,512,2,64]{1,3,2,0:T(8,128)(2,1)S(1)}, u32[]{:S(2)}) copy-start(bf16[1,512,2,64]{1,3,2,0:T(8,128)(2,1)S(1)} %maximum_convert_fusion) | copy-start | bytes 393220
  28.7 9.8 %collective-permute-start = (bf16[2,1,512,128]{3,2,1,0:T(8,128)(2,1)}, bf16[2,1,512,128]{3,2,1,0:T(8,128)(2,1)}, u32[]{:S(2)}, u32[]{:S(2)}) collective-permute-start(bf16[2,1,512,128]{3,2,1,0:T(8,128)(2,1)} %pad_maximum_fusion.5), channel_id=1, source_target_pairs={{0,1},{2,3},{4,5},{6,7},{8,9},{10,11},{12,13},{14,15},{16,17},{18,... | collective-permute-start | bytes 786440 | tf_op jit(solution)/shard_map/ppermute | solution.py:20
  53.3 55.2 %copy-start.87 = (f32[960]{0:T(1024)S(1)}, f32[960]{0:T(1024)}, u32[]{:S(2)}) copy-start(f32[960]{0:T(1024)} %param.25) | copy-start | bytes 11524
  53.3 113.8 %all-reduce.20.cloned.1.call-start = ((), (), s32[]{:S(2)}) async-start(), calls=%async_computation.6 | async-start | bytes 1966080 | tf_op jit(solution)/shard_map/psum | solution.py:153
  115.5 144.0 %all-reduce.22.cloned.1.call-start = ((), (), s32[]{:S(2)}) async-start(), calls=%async_computation.7 | async-start | bytes 1966080 | tf_op jit(solution)/shard_map/psum | solution.py:140
  177.8 10.9 %collective-permute-start.1 = (bf16[2,1,512,128]{3,2,1,0:T(8,128)(2,1)}, bf16[2,1,512,128]{3,2,1,0:T(8,128)(2,1)}, u32[]{:S(2)}, u32[]{:S(2)}) collective-permute-start(bf16[2,1,512,128]{3,2,1,0:T(8,128)(2,1)} %pad_maximum_fusion.6), channel_id=1, source_target_pairs={{0,1},{2,3},{4,5},{6,7},{8,9},{10,11},{12,13},{14,15},{16,17},{18,... | collective-permute-start | bytes 786440 | tf_op jit(solution)/shard_map/ppermute | solution.py:20
  206.8 115.4 %all-reduce.24.cloned.1.call-start = ((), (), s32[]{:S(2)}) async-start(), calls=%async_computation.8 | async-start | bytes 1966080 | tf_op jit(solution)/shard_map/psum | solution.py:217
  270.6 139.7 %all-reduce.26.cloned.1.call-start = ((), (), s32[]{:S(2)}) async-start(), calls=%async_computation.9 | async-start | bytes 1966080 | tf_op jit(solution)/shard_map/psum | solution.py:280
  271.4 54.0 %copy-start.95 = (f32[512]{0:T(512)S(1)}, f32[512]{0:T(512)}, u32[]{:S(2)}) copy-start(f32[512]{0:T(512)} %copy-done.94) | copy-start | bytes 6148
  352.2 3.9 collective-permute-start.2
  359.2 53.9 %copy-start.93 = (f32[512]{0:T(512)S(1)}, f32[512]{0:T(512)}, u32[]{:S(2)}) copy-start(f32[512]{0:T(512)} %copy-done.92) | copy-start | bytes 6148
  359.2 113.4 %all-reduce.28.cloned.1.call-start = ((), (), s32[]{:S(2)}) async-start(), calls=%async_computation.10 | async-start | bytes 1966080 | tf_op jit(solution)/shard_map/psum | solution.py:217
  421.0 100.3 %reduce-scatter.12.cloned.1.call-start = ((), (), s32[]{:S(2)}) async-start(), calls=%async_computation.16 | async-start | bytes 1843200 | tf_op jit(solution)/shard_map/reduce_scatter | solution.py:363
  425.5 95.8 %reduce-scatter.10.cloned.1.call-start = ((), (), s32[]{:S(2)}) async-start(), calls=%async_computation.14 | async-start | bytes 1843200 | tf_op jit(solution)/shard_map/reduce_scatter | solution.py:360
  430.0 91.3 %reduce-scatter.14.cloned.1.call-start = ((), (), s32[]{:S(2)}) async-start(), calls=%async_computation.18 | async-start | bytes 1966080 | tf_op jit(solution)/shard_map/reduce_scatter | solution.py:366
  438.7 85.0 %reduce-scatter.8.cloned.1.call-start = ((), (), s32[]{:S(2)}) async-start(), calls=%async_computation.13 | async-start | bytes 1179648 | tf_op jit(solution)/shard_map/reduce_scatter | solution.py:357
  475.6 14.4 %slice-start = ((s8[12582912]{0:T(1024)(128)(4,1)}), s8[4194304]{0:T(1024)(128)(4,1)S(1)}, s32[]{:S(2)}) async-start(s8[12582912]{0:T(1024)(128)(4,1)} %bitcast.328), calls=%async_computation.22 | async-start | bytes 8388608
  478.0 30.7 %copy-start.11 = (f32[1,512,960]{1,2,0:T(8,128)}, f32[1,512,960]{1,2,0:T(8,128)S(1)}, u32[]{:S(2)}) copy-start(f32[1,512,960]{1,2,0:T(8,128)S(1)} %fusion.43) | copy-start | bytes 5898244
  505.1 11.6 %collective-permute-start.3 = (bf16[2,1,512,128]{2,3,1,0:T(8,128)(2,1)}, bf16[2,1,512,128]{2,3,1,0:T(8,128)(2,1)}, u32[]{:S(2)}, u32[]{:S(2)}) collective-permute-start(bf16[2,1,512,128]{2,3,1,0:T(8,128)(2,1)} %pad_maximum_fusion.8), channel_id=1, source_target_pairs={{1,0},{3,2},{5,4},{7,6},{9,8},{11,10},{13,12},{15,14},{17,16},{19,... | collective-permute-start | bytes 786440 | tf_op jit(solution)/shard_map/ppermute | solution.py:20
  515.2 21.0 %reduce-scatter.6.cloned.1.call-start = ((), (), s32[]{:S(2)}) async-start(), calls=%async_computation.11 | async-start | bytes 1843200 | tf_op jit(solution)/shard_map/reduce_scatter | solution.py:354
  521.2 129.4 %all-reduce.32.cloned.1.call-start = ((), (), s32[]{:S(2)}) async-start(), calls=%async_computation.21 | async-start | bytes 5783552 | tf_op jit(solution)/shard_map/psum | solution.py:377
  536.3 186.4 %all-reduce.30.cloned.1.call-start = ((), (), s32[]{:S(2)}) async-start(), calls=%async_computation.20 | async-start | bytes 3932160 | tf_op jit(solution)/shard_map/psum | solution.py:153
  541.3 110.5 %copy-start.100 = (u32[32]{0:T(128)S(1)}, u32[32]{0:T(128)}, u32[]{:S(2)}) copy-start(u32[32]{0:T(128)} %constant.71) | copy-start | bytes 388
  541.3 112.4 %copy-start.98 = (f32[960]{0:T(1024)S(1)}, f32[960]{0:T(1024)}, u32[]{:S(2)}) copy-start(f32[960]{0:T(1024)} %get-tuple-element.44) | copy-start | bytes 11524
  541.4 183.8 %copy-start.99 = (f32[960]{0:T(1024)S(1)}, f32[960]{0:T(1024)}, u32[]{:S(2)}) copy-start(f32[960]{0:T(1024)} %get-tuple-element.48) | copy-start | bytes 11524
  541.4 208.1 %all-gather.7.cloned.1.call-start = ((), (), s32[]{:S(2)}) async-start(), calls=%async_computation.15 | async-start | bytes 1843200 | tf_op jit(solution)/shard_map/all_gather | solution.py:392
  650.6 101.8 %all-gather.9.cloned.1.call-start = ((), (), s32[]{:S(2)}) async-start(), calls=%async_computation.17 | async-start | bytes 1843200 | tf_op jit(solution)/shard_map/all_gather | solution.py:395
  650.7 74.6 %copy-start.91 = (f32[512]{0:T(512)S(1)}, f32[512]{0:T(512)}, u32[]{:S(2)}) copy-start(f32[512]{0:T(512)} %copy-done.90) | copy-start | bytes 6148
  651.2 106.9 %all-gather.5.cloned.1.call-start = ((), (), s32[]{:S(2)}) async-start(), calls=%async_computation.12 | async-start | bytes 1843200 | tf_op jit(solution)/shard_map/all_gather | solution.py:386
  651.8 118.3 %all-gather.11.cloned.1.call-start = ((), (), s32[]{:S(2)}) async-start(), calls=%async_computation.19 | async-start | bytes 1966080 | tf_op jit(solution)/shard_map/all_gather | solution.py:398
  (107 other events, 341.9 us)
Sparse Core Ops, SparseCore 0:
  53.5 53.3 all-reduce.17
  115.6 51.4 all-reduce.19
  206.9 52.4 all-reduce.21
  270.7 51.4 all-reduce.23
  359.3 50.9 all-reduce.25
  421.1 51.4 all-reduce.27
  474.9 9.4 reduce-scatter.11
  486.6 9.8 reduce-scatter.9
  499.3 9.9 reduce-scatter.13
  515.3 8.3 reduce-scatter.7
  526.6 9.6 reduce-scatter.5
  538.9 111.6 all-reduce.31
  654.3 68.2 all-reduce.29
  724.0 10.1 all-gather.6
  735.6 10.4 all-gather.8
  747.6 10.4 all-gather.4
  759.5 10.5 all-gather.10
where the time goes:
time: 790 us; the launch traced here: 780 us
  waiting for transfers between devices  499 us (63%)
  matrix products  100 us (13%)
  other arithmetic  73.4 us (9%)
  local copies, waits for them, and re-layouts  58.2 us (7%)
  between operations  22 us (3%)
  blocking collectives  16.1 us (2%)
  starting transfers between devices  10.7 us (1%)
    psum x2, waiting for transfers between devices, forward_pass(): lax.psum(feedforward_portion.astype(jnp.bfloat16), 'head')  120 us
    psum x1, waiting for transfers between devices, body(): lax.psum(shares[0].astype(jnp.bfloat16), 'batch').astype(jnp.float32)  109 us
    psum x2, waiting for transfers between devices, forward_pass(): lax.psum(attention_portion.astype(jnp.bfloat16), 'head').astype(jnp.float32)  105 us
    psum x2, waiting for transfers between devices, backward_pass(): lax.psum(feedforward_addend.astype(jnp.bfloat16), 'head')  84.5 us
    psum x1, waiting for transfers between devices, backward_pass(): lax.psum(attention_addend.astype(jnp.bfloat16), 'head').astype(jnp.float32)  50.9 us
    unnamed x241, local copies, waits for them, and re-layouts  24.5 us
    dot_general x2, matrix products, backward_pass(): jnp.einsum('bqsge,bkse->bsgqk', attention_result_gradient, values_all, pr...  21.8 us
    another operation x10, other arithmetic  17.1 us
  transfers between devices with their start and end apart: 21, of which 13 were waited for; matrix products, arithmetic and copies ran while one was open for 13% of the time, Pallas kernels for 0%

commit v1 on v0

v1 whole, which is shorter than its diff:
```python
import functools
import math
from types import SimpleNamespace

import jax
import jax.numpy as jnp
import numpy as np
from jax import lax
from jax.experimental import pallas as pl
from jax.experimental.pallas import tpu as pltpu
from jax.sharding import PartitionSpec as P

KV = 5
HD = 64
GQ = 3
QH = KV * GQ
HEADS = 4
EPS = 1e-05
NEG = -1e30
MESH = pl.DeviceIdType.MESH
F32 = jnp.float32
BF16 = jnp.bfloat16


def nn(a, b):
    return lax.dot_general(a, b, (((1,), (0,)), ((), ())), preferred_element_type=F32)


def nt(a, b):
    return lax.dot_general(a, b, (((1,), (1,)), ((), ())), preferred_element_type=F32)


def tn(a, b):
    return lax.dot_general(a, b, (((0,), (0,)), ((), ())), preferred_element_type=F32)


def rope_table(slots):
    inverse = np.exp(np.arange(HD // 2, dtype=np.float32) * np.float32(-2.0 * math.log(10000.0) / HD))
    angles = np.arange(slots, dtype=np.float32)[:, None] * inverse[None, :].astype(np.float32)
    cos, sin = np.cos(angles).astype(np.float32), np.sin(angles).astype(np.float32)
    return np.concatenate([cos] * 4 + [sin] * 4, axis=1)


def peer_of(h, j):
    return (h, h + 1 - 2 * (h % 2), (h + 2) % 4, 3 - h)[j]


def scratch_of(rows, d, ff, nb):
    n = HEADS
    half = n * rows
    keys = 2 * half
    dp = -(-d // 128) * 128
    kp = -(-KV * HD // 128) * 128
    cr = d // 8
    v = pltpu.VMEM
    dma = pltpu.SemaphoreType.DMA
    return dict(
        hid_v=v((d, rows), BF16),
        cot_v=v((d, half), BF16),
        tab_v=v((rows, 256), F32),
        gains_v=v((2, d), F32),
        wq_v=v((d, QH * HD), BF16),
        wk_v=v((KV * HD, d), BF16),
        wv_v=v((KV * HD, d), BF16),
        wo_v=v((QH * HD, d), BF16),
        wf=v((3 * d, ff), BF16),
        res=v((2, rows, d), F32),
        mid=v((2, rows, d), F32),
        nat=v((d, 2 * rows), BF16),
        dat=v((d, 2 * rows), BF16),
        ql=v((2, KV, GQ * rows, 128), BF16),
        kv=v((2, KV, keys, 128), BF16),
        lse=v((2, rows, 128), F32),
        at=v((rows, d), BF16),
        nf=v((2, n, rows, d), BF16),
        gate=v((2, n, rows, ff), F32),
        up=v((2, n, rows, ff), F32),
        act=v((n, rows, ff), BF16),
        bias=v((rows, keys), F32),
        wide=v((rows, dp), F32),
        wide2=v((rows, kp), F32),
        wide3=v((rows, kp), F32),
        heads=v((QH, rows, 128), F32),
        part=v((rows, d), F32),
        psend=v((3, rows, d), BF16),
        precv=v((2, 3, rows, d), BF16),
        d_res=v((rows, d), F32),
        d_mid=v((rows, d), F32),
        df=v((2, n, rows, d), BF16),
        dg=v((n, rows, ff), BF16),
        du=v((n, rows, ff), BF16),
        ou=v((KV, GQ * rows, 128), BF16),
        dq=v((rows, d), BF16),
        dk=v((rows, KV * HD), BF16),
        dv=v((rows, KV * HD), BF16),
        dpg=v((KV, 2 * rows, 384), BF16),
        aog=v((KV, 2 * rows, 256), BF16),
        dkv=v((KV, 128, half), F32),
        dkv_ctx=v((KV, 128, half), BF16),
        dkv_ctx_r=v((2, KV, 128, half), BF16),
        dkv_s=v((3, KV, 128, rows), BF16),
        dkv_r=v((3, KV, 128, rows), BF16),
        fin=v((2, d, rows), BF16),
        gown=v((12, cr, ff), F32),
        sf=v((12, cr, ff), BF16),
        rf=v((12, cr, ff), BF16),
        rf2=v((12, cr, ff), BF16),
        zs=v((16, cr, ff), BF16),
        zu=v((16, cr, ff), BF16),
        zb=v((16, cr, ff), BF16),
        ha=v((KV, d // 2, 512), BF16),
        ra=v((KV, d // 2, 512), BF16),
        gain_v=v((2, d), F32),
        gain_p=v((2 * n, 2, d), F32),
        gain_z=v((nb, 2, d), F32),
        in_sem=dma((11,)),
        loc_sem=dma((8,)),
        kv_ss=dma((2, 4)),
        kv_rs=dma((2, 4)),
        kvc_ss=dma((2, 4)),
        kvc_rs=dma((2, 4)),
        nf_ss=dma((2, 4)),
        nf_rs=dma((2, 4)),
        p_ss=dma((4, 4)),
        p_rs=dma((4, 4)),
        df_ss=dma((4,)),
        df_rs=dma((4,)),
        dc_ss=dma((2,)),
        dc_rs=dma((2,)),
        dkv_ss=dma((2, 4)),
        dkv_rs=dma((2, 4)),
        fin_ss=dma((2, 4)),
        fin_rs=dma((2, 4)),
        f_ss=dma((3,)),
        f_rs=dma((3,)),
        z_s0=dma((16,)),
        z_s1=dma((16,)),
        z_ur=dma((16,)),
        z_br=dma((16,)),
        og_loc=dma((16,)),
        og_ss=dma((16,)),
        og_rs=dma((16,)),
        a_ss=dma((KV,)),
        a_rs=dma((KV,)),
        h_ss=dma((4,)),
        h_rs=dma((4,)),
        ex_loc=dma((4,)),
        ex_ss=dma((4, 8)),
        ex_rs=dma((4, 8)),
        gp_ss=dma((8,)),
        gp_rs=dma((8,)),
        gz_ss=dma((nb,)),
        gz_rs=dma((nb,)),
    )


def step_kernel(names, rows, d, ff, nb, *refs):
    r = SimpleNamespace(**dict(zip(names, refs)))
    wg_v, wu_v, wd_v = (r.wf.at[pl.ds(t * d, d)] for t in range(3))
    lhs = r.cot_v
    h = lax.axis_index("head")
    c = lax.axis_index("ctx")
    z = lax.axis_index("batch")
    half = HEADS * rows
    hd2 = d // 2
    cr = d // 8
    lane = lax.broadcasted_iota(jnp.int32, (rows, 128), 1)
    low = lane < HD
    quarter = (lane % HD) < HD // 2

    def copy_to(src, dst, ss, rs, where):
        return pltpu.make_async_remote_copy(
            src_ref=src, dst_ref=dst, send_sem=ss, recv_sem=rs, device_id=where, device_id_type=MESH
        )

    def remote(src, dst, ss, rs, j):
        return copy_to(src, dst, ss, rs, dict(head=peer_of(h, j)))

    def across(src, dst, ss, rs):
        return copy_to(src, dst, ss, rs, dict(ctx=1 - c))

    def load(k, src, dst):
        return pltpu.make_async_copy(src, dst, r.in_sem.at[k])

    my_rows = pl.ds(pl.multiple_of(h * rows, rows), rows)
    my_pos = pl.ds(pl.multiple_of(c * half + h * rows, rows), rows)
    loads = SimpleNamespace(
        hid=load(0, r.hid.at[:, my_rows], r.hid_v),
        gains=load(1, r.gains, r.gains_v),
        wk=load(3, r.wk, r.wk_v),
        wv=load(4, r.wv, r.wv_v),
        tab=load(5, r.tab.at[my_pos], r.tab_v),
        wq=load(2, r.wq, r.wq_v),
        wo=load(6, r.wo, r.wo_v),
        wg=load(7, r.wg, wg_v),
        wu=load(8, r.wu, wu_v),
        wd=load(9, r.wd, wd_v),
        cot=load(10, r.cot, r.cot_v),
    )
    for cp in vars(loads).values():
        cp.start()

    plane = [(j, x) for j in range(HEADS) for x in range(2) if (j, x) != (0, 0)]

    def plane_id(j, x):
        return dict(head=peer_of(h, j), ctx=1 - c if x else c)

    barrier = pltpu.get_barrier_semaphore()
    for j, x in plane:
        pl.semaphore_signal(barrier, inc=1, device_id=plane_id(j, x), device_id_type=MESH)
    for k in range(1, nb):
        pl.semaphore_signal(barrier, inc=1, device_id=dict(batch=(z + k) % nb), device_id_type=MESH)
    pl.semaphore_wait(barrier, len(plane) + nb - 1)

    length = r.len[0]
    row_pos = c * half + h * rows + lax.broadcasted_iota(jnp.int32, (rows, 1), 0)
    valid = (row_pos < length).astype(F32)

    for blk in range(2 * HEADS):
        own = blk < HEADS
        base = (c if own else 1 - c) * half + peer_of(h, blk % HEADS) * rows
        kp = base + lax.broadcasted_iota(jnp.int32, (rows, rows), 1)
        qp = c * half + h * rows + lax.broadcasted_iota(jnp.int32, (rows, rows), 0)
        ok = (kp <= qp) & (kp < length)
        r.bias[:, blk * rows : (blk + 1) * rows] = jnp.where(ok, 0.0, NEG)

    zero_w = jnp.zeros((rows, 128), F32)
    dp, kw = r.wide.shape[1], r.wide2.shape[1]
    r.wide[:, dp - 128 :] = zero_w
    r.wide2[:, kw - 128 :] = zero_w
    r.wide3[:, kw - 128 :] = zero_w
    r.lse[0] = zero_w
    r.lse[1] = zero_w

    @pl.when(c == 0)
    def _():
        for p in range(2):
            r.kv[p, :, half:, :] = jnp.zeros((KV, half, 128), BF16)

    def rms(x, gain):
        inv = lax.rsqrt(jnp.mean(x * x, axis=-1, keepdims=True) + EPS)
        return x * inv * gain

    def turned(x):
        return jnp.where(quarter, -pltpu.roll(x, 128 - HD // 2, 1), pltpu.roll(x, HD // 2, 1))

    def rope(x):
        return x * r.tab_v[:, 0:128] + turned(x) * r.tab_v[:, 128:256]

    def unrope(x):
        return x * r.tab_v[:, 0:128] - turned(x) * r.tab_v[:, 128:256]

    def swap(x):
        return pltpu.roll(x, HD, 1)

    def blocks(width):
        return [(b, b * 128, min(128, width - b * 128)) for b in range(-(-width // 128))]

    def head_row(i):
        return i // GQ, (i % GQ) * rows

    def store_t(dst, src):
        for b, lo, w in blocks(d):
            dst[lo : lo + w, :] = src[:, lo : lo + w].T

    gain_a = lambda: r.gains_v[0:1, :]
    gain_f = lambda: r.gains_v[1:2, :]

    loads.tab.wait()
    loads.gains.wait()
    loads.hid.wait()
    for b, lo, w in blocks(d):
        r.res[0, :, lo : lo + w] = r.hid_v[lo : lo + w, :].astype(F32).T

    def forward(p):
        x = r.res[p]
        na = rms(x, gain_a()).astype(BF16)
        store_t(r.nat.at[:, p * rows : (p + 1) * rows], na)
        if p == 0:
            loads.wk.wait()
            loads.wv.wait()
        r.wide2[:, : KV * HD] = nt(na, r.wk_v[...])
        r.wide3[:, : KV * HD] = nt(na, r.wv_v[...])
        for b in range(-(-KV // 2)):
            kb = rope(r.wide2[:, b * 128 : (b + 1) * 128])
            vb = r.wide3[:, b * 128 : (b + 1) * 128]
            r.kv[p, 2 * b, 0:rows, :] = jnp.where(low, kb, swap(vb)).astype(BF16)
            if 2 * b + 1 < KV:
                r.kv[p, 2 * b + 1, 0:rows, :] = jnp.where(low, swap(kb), vb).astype(BF16)
        sends = []
        for j in (1, 2, 3):
            cp = remote(
                r.kv.at[p, :, pl.ds(0, rows)], r.kv.at[p, :, pl.ds(j * rows, rows)],
                r.kv_ss.at[p, j], r.kv_rs.at[p, j], j,
            )
            cp.start()
            sends.append(cp)

        def to_partner(j):
            return across(
                r.kv.at[p, :, pl.ds(j * rows, rows)], r.kv.at[p, :, pl.ds(half + j * rows, rows)],
                r.kvc_ss.at[p, j], r.kvc_rs.at[p, j],
            )

        @pl.when(c == 0)
        def _():
            to_partner(0).start()

        if p == 0:
            loads.wq.wait()
        r.wide[:, :d] = nn(na, r.wq_v[...])
        for b, lo, w in blocks(d):
            y = rope(r.wide[:, lo : lo + 128]).astype(BF16).astype(F32) * HD ** (-0.5)
            g, o = head_row(2 * b)
            r.ql[p, g, o : o + rows, :] = jnp.where(low, y, 0.0).astype(BF16)
            if 2 * b + 1 < QH:
                g, o = head_row(2 * b + 1)
                r.ql[p, g, o : o + rows, :] = jnp.where(low, swap(y), 0.0).astype(BF16)

        for j in (1, 2, 3):
            sends[j - 1].wait_recv()

            @pl.when(c == 0)
            def _():
                to_partner(j).start()

        @pl.when(c == 1)
        def _():
            for j in range(HEADS):
                to_partner(j).wait_recv()

        @pl.loop(0, KV)
        def _(g):
            kv = r.kv[p, g]
            for k in range(GQ):
                s = nt(r.ql[p, g, k * rows : (k + 1) * rows, :], kv)
                s = jnp.where(r.bias[...] < 0.0, NEG, s)
                m = jnp.max(s, axis=-1, keepdims=True)
                e = jnp.exp(s - m)
                t = jnp.sum(e, axis=-1, keepdims=True)
                r.lse[p] += jnp.where(lane == g * GQ + k, m + jnp.log(t), 0.0)
                r.heads[g * GQ + k] = nn((e / t).astype(BF16), kv)

        mine = pl.ds(p * rows, rows)
        for g in range(KV):
            o0, o1, o2 = (r.heads[g * GQ + k] for k in range(GQ))
            r.aog[g, mine, 0:128] = jnp.where(low, 0.0, o0).astype(BF16)
            r.aog[g, mine, 128:256] = jnp.where(low, swap(o1), o2).astype(BF16)
        for b, lo, w in blocks(d):
            first = swap(r.heads[2 * b])
            both = jnp.where(low, first, r.heads[2 * b + 1]) if 2 * b + 1 < QH else first
            r.at[:, lo : lo + w] = both[:, :w].astype(BF16)
        if p == 0:
            loads.wo.wait()
        mid = r.res[p] + nn(r.at[...], r.wo_v[...])
        r.mid[p] = mid
        r.nf[p, 0] = rms(mid, gain_f()).astype(BF16)
        ag = []
        for j in (1, 2, 3):
            cp = remote(r.nf.at[p, 0], r.nf.at[p, j], r.nf_ss.at[p, j], r.nf_rs.at[p, j], j)
            cp.start()
            ag.append(cp)
        if p == 0:
            loads.wg.wait()
            loads.wu.wait()
            loads.wd.wait()
        rs = []
        for j in range(HEADS):
            if j:
                ag[j - 1].wait_recv()
            nf = r.nf[p, j]
            gate = nn(nf, wg_v[...])
            up = nn(nf, wu_v[...])
            r.gate[p, j] = gate
            r.up[p, j] = up
            act = (gate / (1.0 + jnp.exp(-gate)) * up).astype(BF16)
            part = nt(act, wd_v[...])
            if j == 0:
                r.part[...] = part
            else:
                r.psend[j - 1] = part.astype(BF16)
                cp = remote(r.psend.at[j - 1], r.precv.at[p, j - 1], r.p_ss.at[p, j], r.p_rs.at[p, j], j)
                cp.start()
                rs.append(cp)
        total = r.part[...].astype(BF16).astype(F32)
        for j in (1, 2, 3):
            rs[j - 1].wait_recv()
            total = total + r.precv[p, j - 1].astype(F32)
        result = valid * (r.mid[p] + total)
        if p == 0:
            r.res[1] = result
        else:
            r.d_res[...] = result
        for cp in sends + ag + rs:
            cp.wait_send()

        @pl.when(c == 0)
        def _():
            for j in range(HEADS):
                to_partner(j).wait_send()

    def finish(k, value, out):
        store_t(r.fin.at[k], value.astype(BF16))
        cps = []
        own = pltpu.make_async_copy(r.fin.at[k], out.at[:, my_rows], r.loc_sem.at[k])
        own.start()
        for j in (1, 2, 3):
            cp = remote(r.fin.at[k], out.at[:, my_rows], r.fin_ss.at[k, j], r.fin_rs.at[k, j], j)
            cp.start()
            cps.append(cp)
        return own, cps

    root = nb // 2 - 1 + c
    at_root = z == root
    above = z > root
    below = z < root
    has_u = (below & (z > 0)) | (above & (z < nb - 1)) | (at_root & (root > 0))
    outer = (below & (z > 0)) | (above & (z < nb - 1))
    has_b = at_root & (root < nb - 1)

    def zcopy(src, dst, ss, rs, dz):
        return copy_to(src, dst, ss, rs, dict(batch=z + dz))

    def piece(i, own):
        @pl.when(has_u)
        def _():
            zcopy(r.zu.at[i], r.zu.at[i], r.z_s0.at[i], r.z_ur.at[i], 0).wait_recv()

        @pl.when(has_b)
        def _():
            zcopy(r.zb.at[i], r.zb.at[i], r.z_s0.at[i], r.z_br.at[i], 0).wait_recv()

        @pl.when(jnp.logical_not(has_u))
        def _():
            r.zs[i] = own().astype(BF16)

        @pl.when(has_u & jnp.logical_not(has_b))
        def _():
            r.zs[i] = (own() + r.zu[i].astype(F32)).astype(BF16)

        @pl.when(has_u & has_b)
        def _():
            r.zs[i] = (own() + r.zu[i].astype(F32) + r.zb[i].astype(F32)).astype(BF16)

        @pl.when(below)
        def _():
            zcopy(r.zs.at[i], r.zu.at[i], r.z_s0.at[i], r.z_ur.at[i], 1).start()

        @pl.when(above & (z > root + 1))
        def _():
            zcopy(r.zs.at[i], r.zu.at[i], r.z_s0.at[i], r.z_ur.at[i], -1).start()

        @pl.when(z == root + 1)
        def _():
            zcopy(r.zs.at[i], r.zb.at[i], r.z_s0.at[i], r.z_br.at[i], -1).start()

        @pl.when(at_root)
        def _():
            @pl.when(root > 0)
            def _():
                zcopy(r.zs.at[i], r.zb.at[i], r.z_s0.at[i], r.z_br.at[i], -1).start()

            @pl.when(root < nb - 1)
            def _():
                zcopy(r.zs.at[i], r.zb.at[i], r.z_s1.at[i], r.z_br.at[i], 1).start()

    def og_local(i, src):
        return pltpu.make_async_copy(src.at[i], r.og.at[i // 4, c, i % 4], r.og_loc.at[i])

    def og_across(i, src):
        return across(src.at[i], r.og.at[i // 4, c, i % 4], r.og_ss.at[i], r.og_rs.at[i])

    def ex_local(q, src):
        return pltpu.make_async_copy(src.at[12 + q, :, pl.ds(512, 128)], r.ex.at[h, c, q], r.ex_loc.at[q])

    def ex_plane(q, src, j, x):
        return copy_to(
            src.at[12 + q, :, pl.ds(512, 128)], r.ex.at[h, c, q],
            r.ex_ss.at[q, 2 * j + x], r.ex_rs.at[q, 2 * j + x], plane_id(j, x),
        )

    def spread(i):
        def place(src):
            og_local(i, src).start()
            og_across(i, src).start()
            if isinstance(i, int) and i >= 12:
                ex_local(i - 12, src).start()
                for j, x in plane:
                    ex_plane(i - 12, src, j, x).start()

        @pl.when(jnp.logical_not(at_root))
        def _():
            zcopy(r.zb.at[i], r.zb.at[i], r.z_s1.at[i], r.z_br.at[i], 0).wait_recv()

            @pl.when(below & outer)
            def _():
                zcopy(r.zb.at[i], r.zb.at[i], r.z_s1.at[i], r.z_br.at[i], -1).start()

            @pl.when(above & outer)
            def _():
                zcopy(r.zb.at[i], r.zb.at[i], r.z_s1.at[i], r.z_br.at[i], 1).start()

            place(r.zb)

        @pl.when(at_root)
        def _():
            place(r.zs)

    def ffn_half(t):
        sl = pl.ds(4 * t, 4)
        return across(r.sf.at[sl], r.rf.at[sl], r.f_ss.at[t], r.f_rs.at[t])

    def ffn_piece(i):
        @pl.when(i % 4 == 0)
        def _():
            ffn_half(i // 4).wait_recv()

        piece(i, lambda: r.gown[i] + r.rf[i].astype(F32))

    forward(0)
    forward(1)
    out_own, out_cps = finish(0, r.d_res[...], r.out)

    def norm_bwd(x, gain, dn):
        inv = lax.rsqrt(jnp.mean(x * x, axis=-1, keepdims=True) + EPS)
        u = gain * dn
        dx = inv * u - x * (inv * inv * inv) * jnp.mean(x * u, axis=-1, keepdims=True)
        return dx, jnp.sum(dn * x * inv, axis=0, keepdims=True)

    mine_half = pl.ds(pl.multiple_of(c * hd2, hd2), hd2)
    other_half = pl.ds(pl.multiple_of((1 - c) * hd2, hd2), hd2)

    def backward(p):
        if p == 1:
            loads.cot.wait()
            for j in range(HEADS):
                pr = pl.ds(pl.multiple_of(peer_of(h, j) * rows, rows), rows)
                pos = c * half + peer_of(h, j) * rows + lax.broadcasted_iota(jnp.int32, (rows, 1), 0)
                ok = (pos < length).astype(F32)
                for b, lo, w in blocks(d):
                    block = r.cot_v[lo : lo + w, pr].astype(F32).T * ok
                    r.df[p, j, :, lo : lo + w] = block.astype(BF16)
                    if j == 0:
                        r.d_res[:, lo : lo + w] = block
        else:
            block = r.d_res[...] * valid
            r.d_res[...] = block
            r.df[p, 0] = block.astype(BF16)
        ag = []
        if p == 0:
            for j in (1, 2, 3):
                cp = remote(r.df.at[p, 0], r.df.at[p, j], r.df_ss.at[j], r.df_rs.at[j], j)
                cp.start()
                ag.append(cp)
        rs = []
        e = 3 - p
        for j in (1, 2, 3, 0) if p == 1 else (0, 1, 2, 3):
            if p == 0 and j:
                ag[j - 1].wait_recv()
            d_act = nn(r.df[p, j], wd_v[...])
            gate, up = r.gate[p, j], r.up[p, j]
            s = 1.0 / (1.0 + jnp.exp(-gate))
            dg = (d_act * up * s * (1.0 + gate * (1.0 - s))).astype(BF16)
            du = (d_act * (gate * s)).astype(BF16)
            r.act[j] = (gate * s * up).astype(BF16)
            r.dg[j] = dg
            r.du[j] = du
            part = nt(dg, wg_v[...]) + nt(du, wu_v[...])
            if j == 0:
                r.part[...] = part
            else:
                r.psend[j - 1] = part.astype(BF16)
                cp = remote(r.psend.at[j - 1], r.precv.at[1 - p, j - 1], r.p_ss.at[e, j], r.p_rs.at[e, j], j)
                cp.start()
                rs.append(cp)
        for t, rhs in ((0, r.dg), (1, r.du), (2, r.act)):
            if t != 1:
                src = r.nf if t == 0 else r.df
                for j in range(HEADS):
                    store_t(lhs.at[:, j * rows : (j + 1) * rows], src[p, j])
            right = rhs[...].reshape(half, ff)
            theirs = nn(lhs[other_half, :], right)
            for q in range(4):
                v = theirs[q * cr : (q + 1) * cr]
                if p == 0:
                    v = v + r.sf[4 * t + q].astype(F32)
                r.sf[4 * t + q] = v.astype(BF16)
            if p == 0:
                ffn_half(t).start()
            ours = nn(lhs[mine_half, :], right)
            for q in range(4):
                v = ours[q * cr : (q + 1) * cr]
                if p == 0:
                    v = v + r.gown[4 * t + q]
                r.gown[4 * t + q] = v
        dn = r.part[...].astype(BF16).astype(F32)
        for j in (1, 2, 3):
            rs[j - 1].wait_recv()
            dn = dn + r.precv[1 - p, j - 1].astype(F32)
        dx, dgain = norm_bwd(r.mid[p], gain_f(), dn)
        d_mid = r.d_res[...] + dx
        r.d_mid[...] = d_mid
        if p == 1:
            r.gain_v[1:2, :] = dgain
        else:
            r.gain_v[1:2, :] += dgain
        da = d_mid.astype(BF16)
        store_t(r.dat.at[:, p * rows : (p + 1) * rows], da)
        r.wide[:, :d] = nt(da, r.wo_v[...])
        for b, lo, w in blocks(d):
            y = r.wide[:, lo : lo + 128]
            g, o = head_row(2 * b)
            r.ou[g, o : o + rows, :] = jnp.where(low, 0.0, swap(y)).astype(BF16)
            if 2 * b + 1 < QH:
                g, o = head_row(2 * b + 1)
                r.ou[g, o : o + rows, :] = jnp.where(low, 0.0, y).astype(BF16)

        @pl.loop(0, KV)
        def _(g):
            kv = r.kv[p, g]
            acc = None
            for k in range(GQ):
                q = r.ql[p, g, k * rows : (k + 1) * rows, :]
                o = r.ou[g, k * rows : (k + 1) * rows, :]
                s = nt(q, kv)
                s = jnp.where(r.bias[...] < 0.0, NEG, s)
                lse = jnp.sum(jnp.where(lane == g * GQ + k, r.lse[p], 0.0), axis=-1, keepdims=True)
                pr = jnp.exp(s - lse)
                dpr = nt(o, kv)
                delta = jnp.sum(pr * dpr, axis=-1, keepdims=True)
                ds = (pr * (dpr - delta)).astype(BF16)
                r.heads[g * GQ + k] = unrope(nn(ds, kv) * HD ** (-0.5))
                t = nn(o.T, pr.astype(BF16)) + nn(q.T, ds)
                acc = t if acc is None else acc + t
            r.dkv[g] = acc[:, :half]
            r.dkv_ctx[g] = acc[:, half:].astype(BF16)
            if p == 0:
                ffn_piece(g)

                @pl.when(g >= 2)
                def _():
                    spread(g - 2)

        hop = across(r.dkv_ctx, r.dkv_ctx_r.at[p], r.dc_ss.at[p], r.dc_rs.at[p])

        @pl.when(c == 1)
        def _():
            hop.start()

        mine = pl.ds(p * rows, rows)
        for b, lo, w in blocks(d):
            y = r.heads[2 * b]
            if 2 * b + 1 < QH:
                y = jnp.where(low, y, swap(r.heads[2 * b + 1]))
            r.dq[:, lo : lo + w] = y[:, :w].astype(BF16)
        for g in range(KV):
            both = jnp.where(low, r.heads[g * GQ], swap(r.heads[g * GQ + 1]))
            r.dpg[g, mine, 0:128] = both.astype(BF16)

        @pl.when(c == 0)
        def _():
            hop.wait_recv()
            r.dkv[...] += r.dkv_ctx_r[p].astype(F32)

        ks = []
        for j in (1, 2, 3):
            r.dkv_s[j - 1] = r.dkv[:, :, j * rows : (j + 1) * rows].astype(BF16)
            cp = remote(r.dkv_s.at[j - 1], r.dkv_r.at[j - 1], r.dkv_ss.at[p, j], r.dkv_rs.at[p, j], j)
            cp.start()
            ks.append(cp)
        r.wide[:, :d] = nt(r.dq[...], r.wq_v[...])
        for j in (1, 2, 3):
            ks[j - 1].wait_recv()
        keys, vals = [], []
        for g in range(KV):
            t = r.dkv[g, :, 0:rows]
            for j in range(3):
                t = t + r.dkv_r[j, g].astype(F32)
            t = t.T
            kt, vt = unrope(t), swap(t)
            keys.append(kt)
            vals.append(t)
            r.dpg[g, mine, 128:256] = jnp.where(low, r.heads[g * GQ + 2], swap(kt)).astype(BF16)
            r.dpg[g, mine, 256:384] = jnp.where(low, vt, 0.0).astype(BF16)
        for b, lo, w in blocks(KV * HD):
            kb, vb = keys[2 * b], swap(vals[2 * b])
            if 2 * b + 1 < KV:
                kb = jnp.where(low, kb, swap(keys[2 * b + 1]))
                vb = jnp.where(low, vb, vals[2 * b + 1])
            r.dk[:, lo : lo + w] = kb[:, :w].astype(BF16)
            r.dv[:, lo : lo + w] = vb[:, :w].astype(BF16)
        dna = r.wide[:, :d] + nn(r.dk[...], r.wk_v[...]) + nn(r.dv[...], r.wv_v[...])
        dx, dgain = norm_bwd(r.res[p], gain_a(), dna)
        r.d_res[...] = r.d_mid[...] + dx
        if p == 1:
            r.gain_v[0:1, :] = dgain
        else:
            r.gain_v[0:1, :] += dgain
        for cp in ag + rs + ks:
            cp.wait_send()

        @pl.when(c == 1)
        def _():
            hop.wait_send()

    backward(1)
    backward(0)
    gin_own, gin_cps = finish(1, r.d_res[...], r.gin)

    me = 2 * h + c
    r.gain_p[me] = r.gain_v[...]
    gp = [copy_to(r.gain_p.at[me], r.gain_p.at[me], r.gp_ss.at[2 * j + x], r.gp_rs.at[2 * j + x], plane_id(j, x))
          for j, x in plane]
    for cp in gp:
        cp.start()

    def a_half(g):
        src = r.wf.at[pl.ds(pl.multiple_of(g * hd2, hd2), hd2), pl.ds(0, 512)]
        return across(src, r.ra.at[g], r.a_ss.at[g], r.a_rs.at[g])

    @pl.loop(0, KV)
    def _(g):
        def product(rows_of):
            first = nn(r.nat[rows_of, :], r.dpg[g])
            second = nn(r.dat[rows_of, :], r.aog[g])
            return first[:, :256], first[:, 256:] + second[:, :128], second[:, 128:]

        def put(dst, parts):
            dst[:, 0:256] = parts[0].astype(BF16)
            dst[:, 256:384] = parts[1].astype(BF16)
            dst[:, 384:512] = parts[2].astype(BF16)

        put(r.wf.at[pl.ds(pl.multiple_of(g * hd2, hd2), hd2)], product(other_half))
        a_half(g).start()
        put(r.ha.at[g], product(mine_half))

    for cp in gp:
        cp.wait_recv()
    total = r.gain_p[0]
    for k in range(1, 2 * HEADS):
        total = total + r.gain_p[k]
    r.gain_z[z] = total
    gz = [copy_to(r.gain_z.at[z], r.gain_z.at[z], r.gz_ss.at[k], r.gz_rs.at[k], dict(batch=(z + k) % nb))
          for k in range(1, nb)]
    for cp in gz:
        cp.start()

    @pl.loop(5, 9)
    def _(i):
        ffn_piece(i)
        spread(i - 2)

    @pl.loop(0, KV)
    def _(g):
        a_half(g).wait_recv()

    def own_share(to, q):
        at = pl.ds(q * cr, cr)
        g0, g1 = r.gid[to], r.gid[HEADS]
        first = r.ha[g0, at, :].astype(F32) + r.ra[g0, at, :].astype(F32)
        cols = pl.ds(pl.multiple_of(to * 128, 128), 128)
        second = r.ha[g1, at, cols].astype(F32) + r.ra[g1, at, cols].astype(F32)
        return jnp.concatenate([first, second], axis=1)

    for t in range(3):
        ffn_half(t).wait_send()

    def head_share(j):
        sl = pl.ds(4 * (j - 1), 4)
        return remote(r.sf.at[sl], r.rf2.at[sl], r.h_ss.at[j], r.h_rs.at[j], j)

    for j in (1, 2, 3):
        for q in range(4):
            r.sf[4 * (j - 1) + q] = own_share(peer_of(h, j), q).astype(BF16)
        head_share(j).start()

    @pl.loop(9, 12)
    def _(i):
        ffn_piece(i)
        spread(i - 2)

    spread(10)
    spread(11)
    for j in (1, 2, 3):
        head_share(j).wait_recv()

    for q in range(4):
        def own(q=q):
            v = own_share(h, q)
            for j in range(3):
                v = v + r.rf2[4 * j + q].astype(F32)
            return v

        piece(12 + q, own)
        if q:
            spread(11 + q)
    spread(15)

    for cp in gz:
        cp.wait_recv()
    total = r.gain_z[0]
    for k in range(1, nb):
        total = total + r.gain_z[k]
    r.gain_v[...] = total
    gains_out = pltpu.make_async_copy(r.gain_v, r.gains_out, r.loc_sem.at[2])
    gains_out.start()

    gains_out.wait()
    for cp in gp + gz:
        cp.wait_send()
    for j in (1, 2, 3):
        head_share(j).wait_send()

    @pl.loop(0, KV)
    def _(g):
        a_half(g).wait_send()

    @pl.loop(0, 16)
    def _(i):
        og_local(i, r.zs).wait()
        og_across(i, r.zs).wait_send()
        og_across(i, r.zs).wait_recv()

        @pl.when(jnp.logical_not(at_root) | (root > 0))
        def _():
            zcopy(r.zs.at[i], r.zs.at[i], r.z_s0.at[i], r.z_ur.at[i], 0).wait_send()

        @pl.when(outer | (at_root & (root < nb - 1)))
        def _():
            zcopy(r.zs.at[i], r.zs.at[i], r.z_s1.at[i], r.z_ur.at[i], 0).wait_send()

    for q in range(4):
        ex_local(q, r.zs).wait()
        for j, x in plane:
            ex_plane(q, r.zs, j, x).wait_send()
            ex_plane(q, r.zs, j, x).wait_recv()
    for own, cps in ((out_own, out_cps), (gin_own, gin_cps)):
        own.wait()
        for cp in cps:
            cp.wait_recv()
            cp.wait_send()


def body(nb, hidden_in, cotangent, lengths, owners, w_query, w_key, w_value, w_output, gate_weight, up_weight, down_weight,
         gain_attn, gain_ffn):
    half, d = hidden_in.shape[1:]
    ff = gate_weight.shape[1]
    rows = half // HEADS
    cr = d // 8
    scratch = scratch_of(rows, d, ff, nb)
    anyspec = pl.BlockSpec(memory_space=pl.ANY)
    smem = pl.BlockSpec(memory_space=pltpu.SMEM)
    sd = jax.ShapeDtypeStruct
    ins = dict(
        hid=anyspec, cot=anyspec, len=smem, gid=smem, gains=anyspec, tab=anyspec,
        wq=anyspec, wk=anyspec, wv=anyspec, wo=anyspec, wg=anyspec, wu=anyspec, wd=anyspec,
    )
    outs = dict(
        out=sd((d, half), BF16), gin=sd((d, half), BF16),
        og=sd((4, 2, 4, cr, ff), BF16), ex=sd((HEADS, 2, 4, cr, 128), BF16), gains_out=sd((2, d), F32),
    )
    names = tuple(ins) + tuple(outs) + tuple(scratch)
    owned = (owners[None, :] == jnp.arange(HEADS, dtype=jnp.int32)[:, None]).astype(jnp.int32)
    group = jnp.arange(KV, dtype=jnp.int32)
    first = jnp.min(jnp.where(owned == 1, group[None, :], KV), axis=1)
    last = jnp.max(jnp.where(owned == 1, group[None, :], -1), axis=1)
    second = jnp.max(jnp.where(last != first, last, -1))
    gid = jnp.concatenate([first, second[None]]).astype(jnp.int32)
    o, gin, og, ex, gains = pl.pallas_call(
        functools.partial(step_kernel, names, rows, d, ff, nb),
        out_shape=tuple(outs.values()),
        in_specs=list(ins.values()),
        out_specs=(anyspec,) * len(outs),
        scratch_shapes=list(scratch.values()),
        compiler_params=pltpu.CompilerParams(
            collective_id=0, has_side_effects=True, vmem_limit_bytes=67043328
        ),
    )(
        hidden_in[0].T, cotangent[0].T, lengths, gid, jnp.stack([gain_attn, gain_ffn]),
        jnp.asarray(rope_table(2 * half)), w_query, w_key.T, w_value.T, w_output, gate_weight, up_weight, down_weight.T,
    )
    og = og.reshape(4, d, ff)
    has_second = jnp.sum(owned[lax.axis_index("head")]) > 1
    slot0 = og[3, :, :512]
    slot1 = ex.reshape(HEADS, d, 128).transpose(1, 0, 2).reshape(d, 512)
    slot1 = jnp.where(has_second, slot1, jnp.zeros_like(slot1))
    gw = GQ * HD
    pair = lambda lo, hi: jnp.concatenate([slot0[:, lo:hi], slot1[:, lo:hi]], axis=1).astype(F32)
    gq, gk, gv, go = pair(0, gw), pair(gw, gw + HD), pair(gw + HD, gw + 2 * HD), pair(gw + 2 * HD, 512)
    return (
        o.T[None], gin.T.astype(F32)[None], gq, gk, gv, go.T,
        og[0].astype(F32), og[1].astype(F32), og[2].astype(F32).T, gains[0], gains[1],
    )


def solution(mesh):
    rep = P()
    io = P("batch", "ctx", None)
    in_specs = (io, io, P("batch"), rep, rep, rep, rep, rep, P(None, "head"), P(None, "head"), P("head", None), rep, rep)
    out_specs = (io, io, P(None, "head"), P(None, "head"), P(None, "head"), P("head", None), P(None, "head"),
                 P(None, "head"), P("head", None), rep, rep)
    return jax.shard_map(
        functools.partial(body, mesh.shape["batch"]), mesh=mesh, in_specs=in_specs, out_specs=out_specs, check_vma=False
    )
```

time: 790 us -> 377 us (0.48)
  waiting for transfers between devices: 499 us -> 0 us
  Pallas kernels: 0 us -> 347 us
  matrix products: 100 us -> 0 us
  other arithmetic: 73.4 us -> 16 us
  local copies, waits for them, and re-layouts: 58.2 us -> 3.82 us
  between operations: 22 us -> 2.45 us
  blocking collectives: 16.1 us -> 0 us
  starting transfers between devices: 10.7 us -> 0 us
    psum x8 -> x0, waiting for transfers between devices: 470 us -> none  [the longest x2 120 us: forward_pass(): lax.psum(feedforward_portion.astype(jnp.bfloat16), 'head')]
    pallas_call x0 -> x1, Pallas kernels: none -> 347 us  [body(): pl.pallas_call(functools.partial(step_kernel, names, rows, d, ff, nb), ou...]
    dot_general x42 -> x0, matrix products: 100 us -> none  [the longest x2 21.8 us: backward_pass(): jnp.einsum('bqsge,bkse->bsgqk', attention_result_gradient, values_all, pr...]
    slice x30 -> x6, local copies, waits for them, and re-layouts: 25.9 us -> 1.69 us  [the longest x1 0.6 us: body(): gains[1]]
    unnamed x241 -> x9, local copies, waits for them, and re-layouts: 24.5 us -> 1.89 us
    reduce_sum x11 -> x1, other arithmetic: 22.2 us -> 0.64 us  [body(): has_second = jnp.sum(owned[lax.axis_index('head')]) > 1]
    another operation x14 -> x1, other arithmetic: 20.3 us -> 1.31 us  [body(): jnp.stack([gain_attn, gain_ffn])]
    reduce_scatter x5 -> x0, waiting for transfers between devices: 15 us -> none  [the longest x1 12.5 us: body(): lax.psum_scatter(g_in.astype(jnp.bfloat16), 'ctx', scatter_dimension=0, t...]
  transfers between devices with their start and end apart: 21 -> 0, of which waited for: 13 -> 0; matrix products, arithmetic and copies ran while one was open for 13% -> 0% of each run, Pallas kernels for 0% -> 0%
where the time goes in v1:
time: 377 us; the launch traced here: 370 us
  Pallas kernels  347 us (92%)
  other arithmetic  16 us (4%)
  local copies, waits for them, and re-layouts  3.82 us (1%)
    pallas_call x1, Pallas kernels, body(): pl.pallas_call(functools.partial(step_kernel, names, rows, d, ff, nb), ou...  347 us

profile of v1, /device:TPU:27, one launch (start us, length us, event | category | flops | bytes accessed | tf_op | source)
XLA Modules:
  0.0 369.7 jit_solution(6127197357241607532)
XLA Ops:
  0.6 0.8 select_reduce_fusion.1
  1.4 0.6 fusion.1
  2.1 1.2 pad_add_fusion.refs_3_
  3.3 1.3 pad_maximum_fusion.refs_4_
  5.3 347.4 %shard_map.221 = (bf16[960,512]{1,0:T(8,128)(2,1)}, bf16[960,512]{1,0:T(8,128)(2,1)}, bf16[4,2,4,120,640]{4,3,2,1,0:T(8,128)(2,1)}, bf16[4,2,4,120,128]{4,3,2,1,0:T(8,128)(2,1)}, f32[2,960]{1,0:T(2,128)}) custom-call(bf16[960,512]{1,0:T(8,128)(2,1)} %bitcast.50, bf16[960,512]{1,0:T(8,128)(2,1)} %bitcast.51, s32[1]{0:T(128)S(6)} %copy.31.refs_2_, ...), custom_call_target="tpu_custom_call" | custom-call | tf_op jit(solution)/shard_map/pallas_call | solution.py:869
  352.7 0.7 fusion
  353.3 0.6 dynamic-slice_reduce_fusion
  354.6 0.0 copy-start
  354.6 1.4 broadcast_select_fusion
  356.0 0.2 copy.29
  356.2 0.1 fusion.6
  356.4 0.9 copy-done
  357.3 0.1 slice_bitcast_fusion
  357.4 0.1 fusion.5
  357.5 1.2 maximum_convert_fusion.1
  358.7 0.2 fusion.4
  358.9 0.2 fusion.3
  359.2 2.1 convert_bitcast_fusion.2
  361.3 0.3 fusion.2
  361.6 2.8 convert_bitcast_fusion
  364.4 0.0 copy-start.3
  364.4 0.0 copy-start.2
  364.4 1.7 bitcast_convert_fusion.1
  366.1 0.0 copy-done.3
  366.1 0.6 fusion.7
  366.7 0.0 copy-done.2
  366.7 0.0 copy-start.1
  366.7 1.5 convert_bitcast_fusion.1
  368.3 0.0 copy-done.1
  368.3 0.9 copy.32
Async XLA Ops:
  354.6 2.7 copy-start
  364.4 1.7 copy-start.3
  364.4 2.3 copy-start.2
  366.7 1.5 copy-start.1
